TPU v7x, 256 devices: a whole 4x4x8 slice. The times are simulated.
256 devices in a mesh: clique: 8 (over y_hi, x), copy: 32 (over z, y_lo, core).
Axes of the slice: x: 4, y: 4 (y_hi: 2, y_lo: 2; y = y_hi * 2 + y_lo), z: 8, core: 2. Of those that a mesh axis runs over, the one named last changes fastest.
Arguments:
- out_grad: bfloat16 [524288, 512], P(('clique', 'copy')), may hold values from -6 to 6
- pre_act: bfloat16 [524288, 512], P(('clique', 'copy')), may hold values from -6 to 6
- batch_count: int32 [256], P(('clique', 'copy')), may hold values from 1024 to 2048, as said below
- layer_two: bfloat16 [512, 512], replicated, may hold values from -0.25 to 0.25
- hot_slots: int32 [524288, 10], P(('clique', 'copy')), may hold values from 0 to 4095
- cold_index: int32 [524288, 15], P(('clique', 'copy')), may hold values from 0 to 2047
- hot_feats: bfloat16 [4096, 768], P('clique'), may hold values from -6 to 6
- cold_feats: bfloat16 [524288, 768], P(('clique', 'copy')), may hold values from -6 to 6
Outputs:
- grad_one: float32 [768, 512], replicated
- grad_two: float32 [512, 512], replicated
Inputs may be any that keep to these rules, and one draw needn't show every extreme that they name: `batch_count`: some device has all 2048 rows live in every draw.
All inputs are finite; a program needn't handle non-finite values.
Results may differ from a plain program's by a relative error of at most 0.015.
Values may be sent and summed in bfloat16 or wider, within the bound.
A program may use at most 128 MiB of HBM per device.

v0:
```python
import jax
import jax.numpy as jnp
from jax import lax
from jax.sharding import PartitionSpec as P


def table_sums(index_cols, row_grad, table_rows, fanout):
    block = min(512, table_rows)
    blocks = table_rows // block
    offsets = jnp.arange(block, dtype=jnp.int32)

    def one_block(start):
        wanted = start + offsets
        counts = jnp.zeros((block, index_cols.shape[0]), jnp.float32)
        for column in range(index_cols.shape[1]):
            counts = counts + (index_cols[:, column][None, :] == wanted[:, None]).astype(
                jnp.float32
            )
        summed = jnp.dot(counts.astype(jnp.bfloat16), row_grad, preferred_element_type=jnp.float32)
        return (summed * (1.0 / fanout)).astype(jnp.bfloat16)

    starts = jnp.arange(blocks, dtype=jnp.int32) * block
    parts = lax.map(one_block, starts)
    return parts.reshape(table_rows, row_grad.shape[1])


def on_device(
    out_grad, pre_act, batch_count, layer_two, hot_slots, cold_index, hot_feats, cold_feats
):
    rows = out_grad.shape[0]
    hot_local = hot_feats.shape[0]
    hot_total = hot_local * lax.axis_size("clique")
    k_hot = hot_slots.shape[1]
    k_cold = cold_index.shape[1]
    fanout = k_hot + k_cold
    cold_rows = cold_feats.shape[0]
    live = (jnp.arange(rows, dtype=jnp.int32) < batch_count[0])[:, None]
    masked = jnp.where(live, out_grad, jnp.zeros_like(out_grad))
    activ = jnp.maximum(pre_act, jnp.zeros_like(pre_act))
    grad_two = jnp.dot(activ.T, masked, preferred_element_type=jnp.float32)
    back = jnp.dot(masked, layer_two.T, preferred_element_type=jnp.float32)
    row_grad = jnp.where(pre_act > 0, back, jnp.zeros_like(back)).astype(jnp.bfloat16)
    hot_part = table_sums(hot_slots, row_grad, hot_total, fanout)
    summed = lax.psum(hot_part, "clique").astype(jnp.float32)
    owned = lax.dynamic_slice_in_dim(summed, lax.axis_index("clique") * hot_local, hot_local, 0)
    cold_part = table_sums(cold_index, row_grad, cold_rows, fanout)
    grad_one = jnp.dot(cold_feats.T, cold_part, preferred_element_type=jnp.float32)
    grad_one = grad_one + jnp.dot(
        hot_feats.T, owned.astype(jnp.bfloat16), preferred_element_type=jnp.float32
    )
    total_one, total_two = lax.psum((grad_one, grad_two), ("clique", "copy"))
    return (total_one, total_two)


def solution(mesh):
    placed = (
        P(("clique", "copy"), None),
        P(("clique", "copy"), None),
        P(("clique", "copy")),
        P(),
        P(("clique", "copy"), None),
        P(("clique", "copy"), None),
        P("clique", None),
        P(("clique", "copy"), None),
    )
    return jax.shard_map(
        on_device, mesh=mesh, in_specs=placed, out_specs=(P(), P()), check_vma=False
    )
```

profile of v0, /device:TPU:2, one launch (start us, length us, event | category | flops | bytes accessed | tf_op | source)
XLA Modules:
  0.0 475.0 jit_solution(12058573302038147682)
XLA Ops:
  8.1 5.2 %select_convert_fusion = bf16[2048,512]{1,0:T(8,128)(2,1)} fusion(bf16[2048,512]{1,0:T(8,128)(2,1)} %param.13, bf16[512,512]{1,0:T(8,128)(2,1)} %param.15, bf16[2048,512]{1,0:T(8,128)(2,1)} %param.12, pred[2048]{0:T(1024)(128)(4,1)S(1)} %iota_compare_fusion), kind=kOutput, calls=%fused_computation.43 | convolution fusion | flops 1077936128 | bytes 6817792 | tf_op jit(solution)/shard_map/dot_general | solution.py:41
  13.2 63.4 %while.23 = (s32[]{:T(128)}, bf16[8,512,512]{2,1,0:T(8,128)(2,1)}, s32[2048,10]{0,1:T(8,128)S(1)}, s32[8]{0:T(128)S(1)}, bf16[2048,512]{1,0:T(8,128)(2,1)}, /*index=5*/s32[]{:T(128)}) while((s32[]{:T(128)}, bf16[8,512,512]{2,1,0:T(8,128)(2,1)}, s32[2048,10]{0,1:T(8,128)S(1)}, s32[8]{0:T(128)S(1)}, bf16[2048,512]{1,0:T(8,128)(2,1)}, ...), condition=%wide.region_3.4_spmd.clone, body=%wide.region_2.3_spmd.clone.sunk | while | flops 1105723904 | bytes 2871893 | solution.py:23
  13.3 0.6 dynamic_slice.22
  14.6 6.6 %fusion.68 = bf16[8,512,512]{2,1,0:T(8,128)(2,1)} fusion(bf16[8,512,512]{2,1,0:T(8,128)(2,1)} %get-tuple-element.278, s32[]{:T(128)} %get-tuple-element.277, bf16[2048,512]{1,0:T(8,128)(2,1)} %get-tuple-element.287, s32[2048]{0:T(1024)S(1)} %bitcast.126, s32[2048]{0:T(1024)S(1)} %bitcast.127, s32[2048]{0:T(1024)S(1)} %bitcast.128, ...), kind=kOutput, calls=%fused_computation.41.clone.1 | convolution fusion | flops 1105723392 | bytes 2705920 | tf_op jit(solution)/shard_map/while/body/eval_jaxpr/dot_general | solution.py:19
  21.2 0.6 dynamic_slice.22
  22.5 6.6 %fusion.68 = bf16[8,512,512]{2,1,0:T(8,128)(2,1)} fusion(bf16[8,512,512]{2,1,0:T(8,128)(2,1)} %get-tuple-element.278, s32[]{:T(128)} %get-tuple-element.277, bf16[2048,512]{1,0:T(8,128)(2,1)} %get-tuple-element.287, s32[2048]{0:T(1024)S(1)} %bitcast.126, s32[2048]{0:T(1024)S(1)} %bitcast.127, s32[2048]{0:T(1024)S(1)} %bitcast.128, ...), kind=kOutput, calls=%fused_computation.41.clone.1 | convolution fusion | flops 1105723392 | bytes 2705920 | tf_op jit(solution)/shard_map/while/body/eval_jaxpr/dot_general | solution.py:19
  29.2 0.6 dynamic_slice.22
  30.4 6.6 %fusion.68 = bf16[8,512,512]{2,1,0:T(8,128)(2,1)} fusion(bf16[8,512,512]{2,1,0:T(8,128)(2,1)} %get-tuple-element.278, s32[]{:T(128)} %get-tuple-element.277, bf16[2048,512]{1,0:T(8,128)(2,1)} %get-tuple-element.287, s32[2048]{0:T(1024)S(1)} %bitcast.126, s32[2048]{0:T(1024)S(1)} %bitcast.127, s32[2048]{0:T(1024)S(1)} %bitcast.128, ...), kind=kOutput, calls=%fused_computation.41.clone.1 | convolution fusion | flops 1105723392 | bytes 2705920 | tf_op jit(solution)/shard_map/while/body/eval_jaxpr/dot_general | solution.py:19
  37.1 0.6 dynamic_slice.22
  38.4 6.6 %fusion.68 = bf16[8,512,512]{2,1,0:T(8,128)(2,1)} fusion(bf16[8,512,512]{2,1,0:T(8,128)(2,1)} %get-tuple-element.278, s32[]{:T(128)} %get-tuple-element.277, bf16[2048,512]{1,0:T(8,128)(2,1)} %get-tuple-element.287, s32[2048]{0:T(1024)S(1)} %bitcast.126, s32[2048]{0:T(1024)S(1)} %bitcast.127, s32[2048]{0:T(1024)S(1)} %bitcast.128, ...), kind=kOutput, calls=%fused_computation.41.clone.1 | convolution fusion | flops 1105723392 | bytes 2705920 | tf_op jit(solution)/shard_map/while/body/eval_jaxpr/dot_general | solution.py:19
  45.0 0.6 dynamic_slice.22
  46.3 6.6 %fusion.68 = bf16[8,512,512]{2,1,0:T(8,128)(2,1)} fusion(bf16[8,512,512]{2,1,0:T(8,128)(2,1)} %get-tuple-element.278, s32[]{:T(128)} %get-tuple-element.277, bf16[2048,512]{1,0:T(8,128)(2,1)} %get-tuple-element.287, s32[2048]{0:T(1024)S(1)} %bitcast.126, s32[2048]{0:T(1024)S(1)} %bitcast.127, s32[2048]{0:T(1024)S(1)} %bitcast.128, ...), kind=kOutput, calls=%fused_computation.41.clone.1 | convolution fusion | flops 1105723392 | bytes 2705920 | tf_op jit(solution)/shard_map/while/body/eval_jaxpr/dot_general | solution.py:19
  52.9 0.6 dynamic_slice.22
  54.2 6.6 %fusion.68 = bf16[8,512,512]{2,1,0:T(8,128)(2,1)} fusion(bf16[8,512,512]{2,1,0:T(8,128)(2,1)} %get-tuple-element.278, s32[]{:T(128)} %get-tuple-element.277, bf16[2048,512]{1,0:T(8,128)(2,1)} %get-tuple-element.287, s32[2048]{0:T(1024)S(1)} %bitcast.126, s32[2048]{0:T(1024)S(1)} %bitcast.127, s32[2048]{0:T(1024)S(1)} %bitcast.128, ...), kind=kOutput, calls=%fused_computation.41.clone.1 | convolution fusion | flops 1105723392 | bytes 2705920 | tf_op jit(solution)/shard_map/while/body/eval_jaxpr/dot_general | solution.py:19
  60.9 0.6 dynamic_slice.22
  62.1 6.6 %fusion.68 = bf16[8,512,512]{2,1,0:T(8,128)(2,1)} fusion(bf16[8,512,512]{2,1,0:T(8,128)(2,1)} %get-tuple-element.278, s32[]{:T(128)} %get-tuple-element.277, bf16[2048,512]{1,0:T(8,128)(2,1)} %get-tuple-element.287, s32[2048]{0:T(1024)S(1)} %bitcast.126, s32[2048]{0:T(1024)S(1)} %bitcast.127, s32[2048]{0:T(1024)S(1)} %bitcast.128, ...), kind=kOutput, calls=%fused_computation.41.clone.1 | convolution fusion | flops 1105723392 | bytes 2705920 | tf_op jit(solution)/shard_map/while/body/eval_jaxpr/dot_general | solution.py:19
  68.8 0.6 dynamic_slice.22
  70.1 6.6 %fusion.68 = bf16[8,512,512]{2,1,0:T(8,128)(2,1)} fusion(bf16[8,512,512]{2,1,0:T(8,128)(2,1)} %get-tuple-element.278, s32[]{:T(128)} %get-tuple-element.277, bf16[2048,512]{1,0:T(8,128)(2,1)} %get-tuple-element.287, s32[2048]{0:T(1024)S(1)} %bitcast.126, s32[2048]{0:T(1024)S(1)} %bitcast.127, s32[2048]{0:T(1024)S(1)} %bitcast.128, ...), kind=kOutput, calls=%fused_computation.41.clone.1 | convolution fusion | flops 1105723392 | bytes 2705920 | tf_op jit(solution)/shard_map/while/body/eval_jaxpr/dot_general | solution.py:19
  77.0 4.6 fusion.41
  81.5 39.8 %while.22 = (s32[]{:T(128)}, bf16[4,512,512]{2,1,0:T(8,128)(2,1)}, s32[2048,15]{0,1:T(8,128)S(1)}, s32[4]{0:T(128)S(1)}, bf16[2048,512]{1,0:T(8,128)(2,1)}, /*index=5*/s32[]{:T(128)}) while((s32[]{:T(128)}, bf16[4,512,512]{2,1,0:T(8,128)(2,1)}, s32[2048,15]{0,1:T(8,128)S(1)}, s32[4]{0:T(128)S(1)}, bf16[2048,512]{1,0:T(8,128)(2,1)}, ...), condition=%wide.region_1.2_spmd.clone, body=%wide.region_0.1_spmd.clone.sunk | while | flops 1121452544 | bytes 2994773 | solution.py:23
  82.2 0.6 iota_add_fusion.4
  82.9 8.6 %fusion.65 = bf16[4,512,512]{2,1,0:T(8,128)(2,1)} fusion(bf16[4,512,512]{2,1,0:T(8,128)(2,1)} %get-tuple-element.260, s32[]{:T(128)} %get-tuple-element.259, bf16[2048,512]{1,0:T(8,128)(2,1)} %get-tuple-element.269, s32[2048]{0:T(1024)S(1)} %bitcast.111, s32[2048]{0:T(1024)S(1)} %bitcast.112, s32[2048]{0:T(1024)S(1)} %bitcast.113, ...), kind=kOutput, calls=%fused_computation.23.clone.1 | convolution fusion | flops 1121452032 | bytes 2746880 | tf_op jit(solution)/shard_map/while/body/eval_jaxpr/dot_general | solution.py:19
  92.2 0.6 iota_add_fusion.4
  92.9 8.6 %fusion.65 = bf16[4,512,512]{2,1,0:T(8,128)(2,1)} fusion(bf16[4,512,512]{2,1,0:T(8,128)(2,1)} %get-tuple-element.260, s32[]{:T(128)} %get-tuple-element.259, bf16[2048,512]{1,0:T(8,128)(2,1)} %get-tuple-element.269, s32[2048]{0:T(1024)S(1)} %bitcast.111, s32[2048]{0:T(1024)S(1)} %bitcast.112, s32[2048]{0:T(1024)S(1)} %bitcast.113, ...), kind=kOutput, calls=%fused_computation.23.clone.1 | convolution fusion | flops 1121452032 | bytes 2746880 | tf_op jit(solution)/shard_map/while/body/eval_jaxpr/dot_general | solution.py:19
  102.8 8.6 %fusion.65 = bf16[4,512,512]{2,1,0:T(8,128)(2,1)} fusion(bf16[4,512,512]{2,1,0:T(8,128)(2,1)} %get-tuple-element.260, s32[]{:T(128)} %get-tuple-element.259, bf16[2048,512]{1,0:T(8,128)(2,1)} %get-tuple-element.269, s32[2048]{0:T(1024)S(1)} %bitcast.111, s32[2048]{0:T(1024)S(1)} %bitcast.112, s32[2048]{0:T(1024)S(1)} %bitcast.113, ...), kind=kOutput, calls=%fused_computation.23.clone.1 | convolution fusion | flops 1121452032 | bytes 2746880 | tf_op jit(solution)/shard_map/while/body/eval_jaxpr/dot_general | solution.py:19
  112.8 8.6 %fusion.65 = bf16[4,512,512]{2,1,0:T(8,128)(2,1)} fusion(bf16[4,512,512]{2,1,0:T(8,128)(2,1)} %get-tuple-element.260, s32[]{:T(128)} %get-tuple-element.259, bf16[2048,512]{1,0:T(8,128)(2,1)} %get-tuple-element.269, s32[2048]{0:T(1024)S(1)} %bitcast.111, s32[2048]{0:T(1024)S(1)} %bitcast.112, s32[2048]{0:T(1024)S(1)} %bitcast.113, ...), kind=kOutput, calls=%fused_computation.23.clone.1 | convolution fusion | flops 1121452032 | bytes 2746880 | tf_op jit(solution)/shard_map/while/body/eval_jaxpr/dot_general | solution.py:19
  121.4 4.6 fusion.50
  126.0 66.5 %all-reduce.4.cloned.1.call-done = bf16[4096,512]{1,0:T(8,128)(2,1)} async-done(((bf16[4096,512]{1,0:T(8,128)(2,1)}), bf16[4096,512]{1,0:T(8,128)(2,1)}) %all-reduce.4.cloned.1.call-update) | async-done | bytes 4194320 | tf_op jit(solution)/shard_map/psum | solution.py:44
  192.5 3.6 add_bitcast_fusion
  196.0 266.8 %all-reduce.6.cloned.1.call-done = (f32[768,512]{0,1:T(8,128)}, f32[512,512]{1,0:T(8,128)}) async-done(((f32[768,512]{0,1:T(8,128)}, f32[512,512]{1,0:T(8,128)}), (f32[768,512]{0,1:T(8,128)}, f32[512,512]{1,0:T(8,128)})) %all-reduce.6.cloned.1.call-update) | async-done | bytes 2621456 | tf_op jit(solution)/shard_map/psum | solution.py:51
  462.9 3.0 copy.10
  465.9 2.3 copy.30
  (41 shorter events, 9.8 us)
Async XLA Ops:
  7.2 114.2 %copy-start = (bf16[2048,768]{1,0:T(8,128)(2,1)S(1)}, bf16[2048,768]{1,0:T(8,128)(2,1)}, u32[]{:S(2)}) copy-start(bf16[2048,768]{1,0:T(8,128)(2,1)} %param.19) | copy-start | bytes 9437188
  7.2 185.3 %all-reduce.4.cloned.1.call-start = ((), (), s32[]{:S(2)}) async-start(), calls=%async_computation | async-start | bytes 8388608 | tf_op jit(solution)/shard_map/psum | solution.py:44
  8.1 5.2 %copy-start.2 = (s32[2048,10]{0,1:T(8,128)S(1)}, s32[2048,10]{0,1:T(8,128)}, u32[]{:S(2)}) copy-start(s32[2048,10]{0,1:T(8,128)} %param.16) | copy-start | bytes 245764
  76.7 4.8 %copy-start.1 = (s32[2048,15]{0,1:T(8,128)S(1)}, s32[2048,15]{0,1:T(8,128)}, u32[]{:S(2)}) copy-start(s32[2048,15]{0,1:T(8,128)} %param.17) | copy-start | bytes 368644
  76.7 386.1 %all-reduce.6.cloned.1.call-start = ((), (), s32[]{:S(2)}) async-start(), calls=%async_computation.1 | async-start | bytes 5242880 | tf_op jit(solution)/shard_map/psum | solution.py:51
Sparse Core Ops, SparseCore 0:
  76.8 115.5 all-reduce.3
  198.6 264.2 all-reduce.5
where the time goes:
time: 476 us; the launch traced here: 475 us
  waiting for transfers between devices  333 us (70%)
  matrix products  105 us (22%)
  between operations  14.9 us (3%)
  local copies, waits for them, and re-layouts  13.6 us (3%)
  other arithmetic  7.56 us (2%)
    psum x1, waiting for transfers between devices, on_device(): total_one, total_two = lax.psum((grad_one, grad_two), ('clique', 'copy'))  267 us
    dot_general x12, matrix products, one_block(): jnp.dot(counts.astype(jnp.bfloat16), row_grad, preferred_element_type=jnp...  87.3 us
    psum x1, waiting for transfers between devices, on_device(): summed = lax.psum(hot_part, 'clique').astype(jnp.float32)  66.5 us
  transfers between devices with their start and end apart: 2, of which 2 were waited for; matrix products, arithmetic and copies ran while one was open for 10% of the time, Pallas kernels for 0%

commit v1 on v0

--- a/solution.py
+++ b/solution.py
@@ -2,6 +2,11 @@
 import jax.numpy as jnp
 from jax import lax
 from jax.sharding import PartitionSpec as P
+
+
+def summed_here(x, name):
+    pieces = lax.all_gather(x, name)
+    return jnp.sum(pieces, axis=0)
 
 
 def table_sums(index_cols, row_grad, table_rows, fanout):
@@ -41,7 +46,7 @@
     back = jnp.dot(masked, layer_two.T, preferred_element_type=jnp.float32)
     row_grad = jnp.where(pre_act > 0, back, jnp.zeros_like(back)).astype(jnp.bfloat16)
     hot_part = table_sums(hot_slots, row_grad, hot_total, fanout)
-    summed = lax.psum(hot_part, "clique").astype(jnp.float32)
+    summed = summed_here(hot_part, "clique").astype(jnp.float32)
     owned = lax.dynamic_slice_in_dim(summed, lax.axis_index("clique") * hot_local, hot_local, 0)
     cold_part = table_sums(cold_index, row_grad, cold_rows, fanout)
     grad_one = jnp.dot(cold_feats.T, cold_part, preferred_element_type=jnp.float32)

time: 476 us -> 717 us (1.51)
  waiting for transfers between devices: 333 us -> 560 us
  other arithmetic: 7.56 us -> 21.7 us
    all_gather x0 -> x1, waiting for transfers between devices: none -> 297 us  [summed_here(): pieces = lax.all_gather(x, name)]
    psum x1 -> x0, waiting for transfers between devices: 66.5 us -> none  [on_device(): summed = lax.psum(hot_part, 'clique').astype(jnp.float32)]
    reduce_sum x0 -> x1, other arithmetic: none -> 14.2 us  [summed_here(): return jnp.sum(pieces, axis=0)]
  transfers between devices with their start and end apart: 2 -> 2, of which waited for: 2 -> 2; matrix products, arithmetic and copies ran while one was open for 10% -> 7% of each run, Pallas kernels for 0% -> 0%
where the time goes in v1:
time: 717 us; the launch traced here: 716 us
  waiting for transfers between devices  560 us (78%)
  matrix products  106 us (15%)
  other arithmetic  21.7 us (3%)
  between operations  14.9 us (2%)
  local copies, waits for them, and re-layouts  13.6 us (2%)
    all_gather x1, waiting for transfers between devices, summed_here(): pieces = lax.all_gather(x, name)  297 us
    psum x1, waiting for transfers between devices, on_device(): total_one, total_two = lax.psum((grad_one, grad_two), ('clique', 'copy'))  263 us
    dot_general x12, matrix products, one_block(): jnp.dot(counts.astype(jnp.bfloat16), row_grad, preferred_element_type=jnp...  87.9 us
  transfers between devices with their start and end apart: 2, of which 2 were waited for; matrix products, arithmetic and copies ran while one was open for 7% of the time, Pallas kernels for 0%

profile of v1, /device:TPU:2, one launch (start us, length us, event | category | flops | bytes accessed | tf_op | source)
XLA Modules:
  0.0 716.1 jit_solution(10865041712418734804)
XLA Ops:
  8.1 5.1 select_convert_fusion
  13.2 63.5 %while.23 = (s32[]{:T(128)}, bf16[8,512,512]{2,1,0:T(8,128)(2,1)}, s32[2048,10]{0,1:T(8,128)S(1)}, s32[8]{0:T(128)S(1)}, bf16[2048,512]{1,0:T(8,128)(2,1)}, /*index=5*/s32[]{:T(128)}) while((s32[]{:T(128)}, bf16[8,512,512]{2,1,0:T(8,128)(2,1)}, s32[2048,10]{0,1:T(8,128)S(1)}, s32[8]{0:T(128)S(1)}, bf16[2048,512]{1,0:T(8,128)(2,1)}, ...), condition=%wide.region_3.4_spmd.clone, body=%wide.region_2.3_spmd.clone.sunk | while | flops 1105723904 | bytes 2871393 | solution.py:28
  13.2 0.6 dynamic_slice.22
  13.9 0.6 iota_add_fusion.5
  14.5 6.6 fusion.68
  21.2 0.6 dynamic_slice.22
  22.4 6.6 fusion.68
  29.1 0.6 dynamic_slice.22
  30.4 6.6 fusion.68
  37.1 0.6 dynamic_slice.22
  38.4 6.6 fusion.68
  45.0 0.6 dynamic_slice.22
  46.3 6.6 fusion.68
  52.9 0.6 dynamic_slice.22
  54.2 6.6 fusion.68
  60.8 0.6 dynamic_slice.22
  62.1 6.6 fusion.68
  68.8 0.6 dynamic_slice.22
  70.0 6.6 fusion.68
  76.9 4.6 fusion.41
  81.5 40.4 %while.22 = (s32[]{:T(128)}, bf16[4,512,512]{2,1,0:T(8,128)(2,1)}, s32[2048,15]{0,1:T(8,128)S(1)}, s32[4]{0:T(128)S(1)}, bf16[2048,512]{1,0:T(8,128)(2,1)}, /*index=5*/s32[]{:T(128)}) while((s32[]{:T(128)}, bf16[4,512,512]{2,1,0:T(8,128)(2,1)}, s32[2048,15]{0,1:T(8,128)S(1)}, s32[4]{0:T(128)S(1)}, bf16[2048,512]{1,0:T(8,128)(2,1)}, ...), condition=%wide.region_1.2_spmd.clone, body=%wide.region_0.1_spmd.clone.sunk | while | flops 1121452544 | bytes 2994273 | solution.py:28
  82.8 8.7 %fusion.65 = bf16[4,512,512]{2,1,0:T(8,128)(2,1)} fusion(bf16[4,512,512]{2,1,0:T(8,128)(2,1)} %get-tuple-element.262, s32[]{:T(128)S(6)} %copy.16, bf16[2048,512]{1,0:T(8,128)(2,1)} %get-tuple-element.271, s32[2048]{0:T(1024)S(1)} %bitcast.111, s32[2048]{0:T(1024)S(1)} %bitcast.112, s32[2048]{0:T(1024)S(1)} %bitcast.113, s32[2048]{0:T(1024)S(1)} %bitcast.114, ...), kind=kOutput, calls=%fused_computation.23.clone.1 | convolution fusion | flops 1121452032 | bytes 2746372 | tf_op jit(solution)/shard_map/while/body/eval_jaxpr/dot_general | solution.py:24
  92.8 9.2 %fusion.65 = bf16[4,512,512]{2,1,0:T(8,128)(2,1)} fusion(bf16[4,512,512]{2,1,0:T(8,128)(2,1)} %get-tuple-element.262, s32[]{:T(128)S(6)} %copy.16, bf16[2048,512]{1,0:T(8,128)(2,1)} %get-tuple-element.271, s32[2048]{0:T(1024)S(1)} %bitcast.111, s32[2048]{0:T(1024)S(1)} %bitcast.112, s32[2048]{0:T(1024)S(1)} %bitcast.113, s32[2048]{0:T(1024)S(1)} %bitcast.114, ...), kind=kOutput, calls=%fused_computation.23.clone.1 | convolution fusion | flops 1121452032 | bytes 2746372 | tf_op jit(solution)/shard_map/while/body/eval_jaxpr/dot_general | solution.py:24
  103.3 8.6 %fusion.65 = bf16[4,512,512]{2,1,0:T(8,128)(2,1)} fusion(bf16[4,512,512]{2,1,0:T(8,128)(2,1)} %get-tuple-element.262, s32[]{:T(128)S(6)} %copy.16, bf16[2048,512]{1,0:T(8,128)(2,1)} %get-tuple-element.271, s32[2048]{0:T(1024)S(1)} %bitcast.111, s32[2048]{0:T(1024)S(1)} %bitcast.112, s32[2048]{0:T(1024)S(1)} %bitcast.113, s32[2048]{0:T(1024)S(1)} %bitcast.114, ...), kind=kOutput, calls=%fused_computation.23.clone.1 | convolution fusion | flops 1121452032 | bytes 2746372 | tf_op jit(solution)/shard_map/while/body/eval_jaxpr/dot_general | solution.py:24
  113.2 8.7 %fusion.65 = bf16[4,512,512]{2,1,0:T(8,128)(2,1)} fusion(bf16[4,512,512]{2,1,0:T(8,128)(2,1)} %get-tuple-element.262, s32[]{:T(128)S(6)} %copy.16, bf16[2048,512]{1,0:T(8,128)(2,1)} %get-tuple-element.271, s32[2048]{0:T(1024)S(1)} %bitcast.111, s32[2048]{0:T(1024)S(1)} %bitcast.112, s32[2048]{0:T(1024)S(1)} %bitcast.113, s32[2048]{0:T(1024)S(1)} %bitcast.114, ...), kind=kOutput, calls=%fused_computation.23.clone.1 | convolution fusion | flops 1121452032 | bytes 2746372 | tf_op jit(solution)/shard_map/while/body/eval_jaxpr/dot_general | solution.py:24
  121.9 4.6 fusion.50
  126.5 297.2 %all-gather.2.cloned.1.call-done = bf16[8,4096,512]{2,1,0:T(8,128)(2,1)} async-done(((bf16[1,4096,512]{2,1,0:T(8,128)(2,1)}), bf16[8,4096,512]{2,1,0:T(8,128)(2,1)}) %all-gather.2.cloned.1.call-update) | async-done | bytes 33554448 | tf_op jit(solution)/shard_map/all_gather | solution.py:8
  423.7 14.2 %reduce_sum.12 = bf16[4096,512]{1,0:T(8,128)(2,1)} reduce(bf16[8,4096,512]{2,1,0:T(8,128)(2,1)} %all-gather.2.cloned.1.call-done, bf16[]{:T(256)} %constant.14.clone.1), dimensions={0}, to_apply=%region_4.5 | reduce | flops 14680064 | bytes 37748736 | tf_op jit(solution)/shard_map/reduce_sum | solution.py:9
  437.9 3.6 add_bitcast_fusion
  441.5 262.5 %all-reduce.3.cloned.1.call-done = (f32[768,512]{0,1:T(8,128)}, f32[512,512]{1,0:T(8,128)}) async-done(((f32[768,512]{0,1:T(8,128)}, f32[512,512]{1,0:T(8,128)}), (f32[768,512]{0,1:T(8,128)}, f32[512,512]{1,0:T(8,128)})) %all-reduce.3.cloned.1.call-update) | async-done | bytes 2621456 | tf_op jit(solution)/shard_map/psum | solution.py:56
  704.0 3.0 copy.11
  707.0 2.3 copy.30
  (42 shorter events, 10.4 us)
Async XLA Ops:
  7.2 114.7 %copy-start = (bf16[2048,768]{1,0:T(8,128)(2,1)S(1)}, bf16[2048,768]{1,0:T(8,128)(2,1)}, u32[]{:S(2)}) copy-start(bf16[2048,768]{1,0:T(8,128)(2,1)} %param.19) | copy-start | bytes 9437188
  7.2 416.5 %all-gather.2.cloned.1.call-start = ((), (), s32[]{:S(2)}) async-start(), calls=%async_computation | async-start | bytes 37748736 | tf_op jit(solution)/shard_map/all_gather | solution.py:8
  8.1 5.1 copy-start.2
  76.7 4.8 copy-start.1
  76.7 627.4 %all-reduce.3.cloned.1.call-start = ((), (), s32[]{:S(2)}) async-start(), calls=%async_computation.1 | async-start | bytes 5242880 | tf_op jit(solution)/shard_map/psum | solution.py:56
Sparse Core Ops, SparseCore 0:
  76.8 346.8 all-gather.1
  441.6 262.3 all-reduce.2
